TPU v7x, 32 devices: a whole 2x2x4 slice. The times are simulated.
32 devices in a mesh: dp: 4 (over z), shard: 8 (over y, x, core).
Axes of the slice: x: 2, y: 2, z: 4, core: 2. Of those that a mesh axis runs over, the one named last changes fastest.
Arguments:
- tokens: bfloat16 [16384, 1024], P(('dp', 'shard')), may hold values from -6 to 6
- targets: bfloat16 [16384, 1024], P(('dp', 'shard')), may hold values from -6 to 6
- segments: int32 [16384], P('dp'), may hold values from 0 to 511, as said below
- valid: int32 [16384], P(('dp', 'shard')), may hold values from 0 to 1, as said below
- master: float32 [1024, 12288], P('shard')
- vectors: float32 [13312], P('shard')
- left_stat: float32 [8, 96, 128, 128], P('shard'), as said below
- right_stat: float32 [8, 96, 128, 128], P('shard'), as said below
- left_root: bfloat16 [8, 96, 128, 128], P('shard'), as said below
- right_root: bfloat16 [8, 96, 128, 128], P('shard'), as said below
- vector_stat: float32 [13312], P('shard'), may hold values from 0.01 to 1
Outputs:
- input_grad: float32 [16384, 1024], P(('dp', 'shard'))
- grad_norm: float32 [], replicated
- new_left: float32 [8, 96, 128, 128], P('shard')
- new_right: float32 [8, 96, 128, 128], P('shard')
- new_master: float32 [1024, 12288], P('shard')
- master_copy: bfloat16 [1024, 12288], P('shard')
- new_vectors: float32 [13312], P('shard')
- new_vector_stat: float32 [13312], P('shard')
Inputs may be any that keep to these rules, and one draw needn't show every extreme that they name: `segments`: taken in order of positions, within each sequence the numbers start at 0 and never fall, rising by at most one from a position to the next; positions 128 to 384 lie in one document, and so do positions 640 to 896. The row of position 0 of every sequence is valid. `left_stat`: every block is symmetric. `right_stat`: every block is symmetric. `left_root`: every block is symmetric. `right_root`: every block is symmetric.
All inputs are finite; a program needn't handle non-finite values.
Results may differ from a plain program's by a relative error of at most 0.012.
Values may be sent and summed in bfloat16 or wider, within the bound.
A program may use at most 320 MiB of HBM per device.

v0:
```python
from functools import partial
import math
import jax
import jax.numpy as jnp
from jax import lax
from jax.sharding import PartitionSpec as P

HD = 64
ROT = 16
BS = 128
EPS = 1e-05
NEG = -1e30
LEARN = 0.5
LEARN_VEC = 0.15
HIGHEST = lax.Precision.HIGHEST


def partner(shard, axis, distance):
    return lax.ppermute(shard, axis, [(i, i ^ 1 << distance) for i in range(lax.axis_size(axis))])


def layer_norm(values, gain, shift):
    row_mean = jnp.mean(values, axis=-1, keepdims=True)
    centred = values - row_mean
    spread = jnp.mean(centred * centred, axis=-1, keepdims=True)
    return centred * lax.rsqrt(spread + EPS) * gain + shift


def rotate(values, cosine_grid, sine_grid):
    half_rot = ROT // 2
    first = values[..., :half_rot]
    second = values[..., half_rot:ROT]
    return jnp.concatenate(
        [
            first * cosine_grid - second * sine_grid,
            second * cosine_grid + first * sine_grid,
            values[..., ROT:],
        ],
        axis=-1,
    )


def angles(positions):
    half_rot = ROT // 2
    frequency = jnp.power(10000.0, -2.0 * jnp.arange(half_rot, dtype=jnp.float32) / ROT)
    angle_grid = positions.astype(jnp.float32)[:, None] * frequency[None, :]
    return (jnp.cos(angle_grid)[:, None, :], jnp.sin(angle_grid)[:, None, :])


def place_rows(parity, row_count):
    half_rows = row_count // 2
    local = jnp.arange(row_count, dtype=jnp.int32)
    block = 2 * parity + local // half_rows
    quarter = jnp.where(block == 0, 0, jnp.where(block == 1, 3, block - 1))
    return quarter * half_rows + local % half_rows


def body(
    tokens,
    targets,
    segments,
    valid,
    master,
    vectors,
    left_stat,
    right_stat,
    left_root,
    right_root,
    vector_stat,
):
    row_count, model_width = tokens.shape
    head_count = model_width // HD
    stack_width = master.shape[1]
    hidden_width = (stack_width - 4 * model_width) // 2
    shard_count = lax.axis_size("shard")
    data_count = lax.axis_size("dp")
    shard_index = lax.axis_index("shard")
    is_later = shard_index % 2
    partner_index = shard_index + 1 - 2 * is_later
    weights, vector_copy = (
        lax.all_gather(master.astype(jnp.bfloat16), "shard", axis=0, tiled=True),
        lax.all_gather(vectors.astype(jnp.bfloat16), "shard", axis=0, tiled=True),
    )
    valid_float = valid.astype(jnp.float32)
    valid_total = lax.psum(jnp.sum(valid_float), ("dp", "shard"))
    params = vector_copy.astype(jnp.float32)
    gain_one = params[0:model_width]
    shift_one = params[model_width : 2 * model_width]
    gain_two = params[2 * model_width : 3 * model_width]
    shift_two = params[3 * model_width : 4 * model_width]
    bias_qkv = params[4 * model_width : 7 * model_width]
    bias_out = params[7 * model_width : 8 * model_width]
    bias_up = params[8 * model_width : 8 * model_width + hidden_width]
    bias_down = params[8 * model_width + hidden_width :]
    w_qkv = weights[:, : 3 * model_width]
    w_out = weights[:, 3 * model_width : 4 * model_width]
    w_up = weights[:, 4 * model_width : 4 * model_width + hidden_width]
    w_down = weights[:, 4 * model_width + hidden_width :]
    inputs = tokens.astype(jnp.float32)
    norm_one, back_one = jax.vjp(layer_norm, inputs, gain_one, shift_one)
    norm_two, back_two = jax.vjp(layer_norm, inputs, gain_two, shift_two)
    one_low = norm_one.astype(jnp.bfloat16)
    two_low = norm_two.astype(jnp.bfloat16)
    projected = jnp.dot(one_low, w_qkv, preferred_element_type=jnp.float32) + bias_qkv
    head_shape = (row_count, head_count, HD)
    positions = place_rows(is_later, row_count)
    partner_pos = place_rows(1 - is_later, row_count)
    cosine_grid, sine_grid = angles(positions)
    turner = partial(rotate, cosine_grid=cosine_grid, sine_grid=sine_grid)
    query_rot, query_back = jax.vjp(turner, projected[:, :model_width].reshape(head_shape))
    key_rot, key_back = jax.vjp(
        turner, projected[:, model_width : 2 * model_width].reshape(head_shape)
    )
    query_low = query_rot.astype(jnp.bfloat16)
    key_low = key_rot.astype(jnp.bfloat16).reshape(row_count, model_width)
    value_low = projected[:, 2 * model_width :].astype(jnp.bfloat16)
    prior_key, prior_value = partner((key_low, value_low), "shard", 0)
    own_ids = lax.dynamic_slice_in_dim(segments, shard_index * row_count, row_count)
    partner_ids = lax.dynamic_slice_in_dim(segments, partner_index * row_count, row_count)
    key_ids = jnp.concatenate([partner_ids, own_ids])
    key_pos = jnp.concatenate([partner_pos, positions])
    allowed = (key_pos[None, :] <= positions[:, None]) & (key_ids[None, :] == own_ids[:, None])
    key_shape = (2 * row_count, head_count, HD)
    key_all = jnp.concatenate([prior_key, key_low], axis=0).reshape(key_shape)
    value_all = jnp.concatenate([prior_value, value_low], axis=0).reshape(key_shape)

    def masked_scores(key_part):
        scores = jnp.einsum(
            "qhe,khe->hqk", query_low, key_part, preferred_element_type=jnp.float32
        ) * HD ** (-0.5)
        return jnp.where(allowed[None], scores, NEG)

    scores = masked_scores(key_all)
    row_max = jnp.max(scores, axis=-1, keepdims=True)
    exponent = jnp.exp(scores - row_max)
    row_sum = jnp.sum(exponent, axis=-1, keepdims=True)
    soft_weights = exponent / row_sum
    attention = jnp.einsum(
        "hqk,khe->qhe",
        soft_weights.astype(jnp.bfloat16),
        value_all,
        preferred_element_type=jnp.float32,
    )
    attention_low = attention.reshape(row_count, model_width).astype(jnp.bfloat16)
    branch = jnp.dot(attention_low, w_out, preferred_element_type=jnp.float32) + bias_out
    up_value = jnp.dot(two_low, w_up, preferred_element_type=jnp.float32) + bias_up
    active, active_back = jax.vjp(partial(jax.nn.gelu, approximate=False), up_value)
    active_low = active.astype(jnp.bfloat16)
    feed_out = (
        jnp.einsum("tf,df->td", active_low, w_down, preferred_element_type=jnp.float32) + bias_down
    )
    outputs = inputs + (branch + feed_out)
    tokens_all = row_count * shard_count * data_count
    grad_out = (
        tokens_all / valid_total * valid_float[:, None] * (outputs - targets.astype(jnp.float32))
    )
    grad_low = grad_out.astype(jnp.bfloat16)
    grad_attention = jnp.einsum("te,de->td", grad_low, w_out, preferred_element_type=jnp.float32)
    grad_attention_low = grad_attention.astype(jnp.bfloat16).reshape(head_shape)
    grad_active = jnp.dot(grad_low, w_down, preferred_element_type=jnp.float32)
    up_low = active_back(grad_active)[0].astype(jnp.bfloat16)
    grad_two = jnp.einsum("tf,df->td", up_low, w_up, preferred_element_type=jnp.float32)
    back_keys, back_values = (key_all, value_all)
    weights_again = jnp.exp(masked_scores(back_keys) - row_max) / row_sum
    grad_weights = jnp.einsum(
        "qhe,khe->hqk", grad_attention_low, back_values, preferred_element_type=jnp.float32
    )
    weighted_sum = jnp.sum(weights_again * grad_weights, axis=-1, keepdims=True)
    grad_scores = (weights_again * (grad_weights - weighted_sum)).astype(jnp.bfloat16)
    grad_query = jnp.einsum(
        "hqk,khe->qhe", grad_scores, back_keys, preferred_element_type=jnp.float32
    ) * HD ** (-0.5)
    grad_keys = jnp.einsum(
        "hqk,qhe->khe", grad_scores, query_low, preferred_element_type=jnp.float32
    ) * HD ** (-0.5)
    grad_values = jnp.einsum(
        "hqk,qhe->khe",
        weights_again.astype(jnp.bfloat16),
        grad_attention_low,
        preferred_element_type=jnp.float32,
    )
    back_key, back_value = (
        partner(
            grad_keys[:row_count].reshape(row_count, model_width).astype(jnp.bfloat16), "shard", 0
        ).astype(jnp.float32),
        partner(
            grad_values[:row_count].reshape(row_count, model_width).astype(jnp.bfloat16), "shard", 0
        ).astype(jnp.float32),
    )
    own_key_grad = grad_keys[row_count:].reshape(row_count, model_width) + back_key
    own_value_grad = grad_values[row_count:].reshape(row_count, model_width) + back_value
    query_pre = query_back(grad_query)[0].reshape(row_count, model_width)
    key_pre = key_back(own_key_grad.reshape(head_shape))[0].reshape(row_count, model_width)
    qkv_low = jnp.concatenate([query_pre, key_pre, own_value_grad], axis=1).astype(jnp.bfloat16)
    grad_one = jnp.einsum("tc,dc->td", qkv_low, w_qkv, preferred_element_type=jnp.float32)
    input_one, gain_one_grad, shift_one_grad = back_one(grad_one)
    input_two, gain_two_grad, shift_two_grad = back_two(grad_two)
    input_grad = grad_out + input_one + input_two
    grad_low_sum = jnp.sum(grad_low.astype(jnp.float32), axis=0)
    vector_grad = jnp.concatenate(
        [
            gain_one_grad,
            shift_one_grad,
            gain_two_grad,
            shift_two_grad,
            jnp.sum(qkv_low.astype(jnp.float32), axis=0),
            grad_low_sum,
            jnp.sum(up_low.astype(jnp.float32), axis=0),
            grad_low_sum,
        ]
    )
    weight_grad = jnp.concatenate(
        [
            jnp.einsum("td,tc->dc", one_low, qkv_low, preferred_element_type=jnp.float32),
            jnp.einsum("td,te->de", attention_low, grad_low, preferred_element_type=jnp.float32),
            jnp.einsum("td,tf->df", two_low, up_low, preferred_element_type=jnp.float32),
            jnp.einsum("te,tf->ef", grad_low, active_low, preferred_element_type=jnp.float32),
        ],
        axis=1,
    )
    spread_vec = vector_grad.reshape(shard_count, data_count, -1).transpose(1, 0, 2).reshape(-1)
    part_weight, part_vector = (
        lax.psum_scatter(weight_grad, "dp", scatter_dimension=1, tiled=True),
        lax.psum_scatter(spread_vec, "dp", scatter_dimension=0, tiled=True),
    )
    part_weight, part_vector = (
        lax.psum_scatter(part_weight, "shard", scatter_dimension=0, tiled=True),
        lax.psum_scatter(part_vector, "shard", scatter_dimension=0, tiled=True),
    )
    own_weight, own_vector = (
        lax.all_gather(part_weight, "dp", axis=1, tiled=True),
        lax.all_gather(part_vector, "dp", axis=0, tiled=True),
    )
    square_sum = jnp.sum(own_weight * own_weight) + jnp.sum(own_vector * own_vector)
    grad_norm = jnp.sqrt(lax.psum(square_sum, "shard"))
    factor = jnp.minimum(1.0, math.sqrt(model_width * stack_width / BS) / grad_norm)
    own_rows = own_weight.shape[0]
    tiles = (own_weight * factor).reshape(own_rows // BS, BS, stack_width // BS, BS)
    new_left = 0.5 * left_stat + 0.5 * jnp.einsum(
        "iajb,icjb->ijac", tiles, tiles, precision=HIGHEST
    )
    new_right = 0.5 * right_stat + 0.5 * jnp.einsum(
        "iajb,iajd->ijbd", tiles, tiles, precision=HIGHEST
    )
    tiles_low = tiles.astype(jnp.bfloat16)
    left_mixed = jnp.einsum(
        "ijac,icjd->iajd", left_root, tiles_low, preferred_element_type=jnp.float32
    ).astype(jnp.bfloat16)
    update = jnp.einsum(
        "iajd,ijdb->iajb", left_mixed, right_root, preferred_element_type=jnp.float32
    ).reshape(own_rows, stack_width)
    new_master = master - LEARN * update
    scaled_vec = own_vector * factor
    new_vstat = 0.5 * vector_stat + 0.5 * scaled_vec * scaled_vec
    new_vectors = vectors - LEARN_VEC * scaled_vec / jnp.sqrt(new_vstat)
    return (
        input_grad,
        grad_norm,
        new_left,
        new_right,
        new_master,
        new_master.astype(jnp.bfloat16),
        new_vectors,
        new_vstat,
    )


def solution(mesh):
    return jax.shard_map(
        body,
        mesh=mesh,
        in_specs=(
            P(("dp", "shard"), None),
            P(("dp", "shard"), None),
            P("dp"),
            P(("dp", "shard")),
            P("shard", None),
            P("shard"),
            P("shard", None, None, None),
            P("shard", None, None, None),
            P("shard", None, None, None),
            P("shard", None, None, None),
            P("shard"),
        ),
        out_specs=(
            P(("dp", "shard"), None),
            P(),
            P("shard", None, None, None),
            P("shard", None, None, None),
            P("shard", None),
            P("shard", None),
            P("shard"),
            P("shard"),
        ),
        check_vma=False,
    )
```

profile of v0, /device:TPU:0, one launch (start us, length us, event | category | flops | bytes accessed | tf_op | source)
XLA Modules:
  0.0 1619.4 jit_solution(14062656077153369523)
XLA Ops:
  12.9 42.6 %psum.14 = f32[]{:T(128)} all-reduce(f32[]{:T(128)} %convert_reduce_fusion.4), channel_id=1, replica_groups=mesh['dp'=4,'shard'=8] {'dp','shard'}, use_global_device_ids=true, to_apply=%region_1.2 | all-reduce | flops 1 | bytes 8 | tf_op jit(solution)/shard_map/psum | solution.py:85
  55.6 10.1 all-gather
  74.0 67.4 %all-gather.4.cloned.1.call-done = bf16[1024,12288]{1,0:T(8,128)(2,1)} async-done(((bf16[128,12288]{1,0:T(8,128)(2,1)}), bf16[1024,12288]{1,0:T(8,128)(2,1)}) %all-gather.4.cloned.1.call-update) | async-done | bytes 25165840 | tf_op jit(solution)/shard_map/all_gather | solution.py:81
  158.4 26.6 %multiply_convert_fusion.1 = (bf16[512,4096]{1,0:T(8,128)(2,1)}, f32[512,4096]{1,0:T(8,128)}, f32[512,4096]{1,0:T(8,128)}) fusion(f32[4096]{0:T(1024)S(1)} %slice.122, bf16[1024,12288]{1,0:T(8,128)(2,1)} %all-gather.4.cloned.1.call-done, bf16[512,1024]{1,0:T(8,128)(2,1)} %param.11, f32[1024]{0:T(1024)S(1)} %get-tuple-element.42, ...), kind=kOutput, calls=%fused_computation.15 | convolution fusion | flops 4436525056 | bytes 30437376 | tf_op jit(solution)/shard_map/dot_general | solution.py:146
  198.7 17.4 %fusion.104 = f32[16,512,1024]{2,1,0:T(8,128)} fusion(bf16[512,16,64]{0,2,1:T(8,128)(2,1)} %maximum_convert_fusion, bf16[512,16,64]{0,2,1:T(8,128)(2,1)} %bitcast.5, bf16[512,16,48]{0,2,1:T(8,128)(2,1)} %slice.168, bf16[512,16,8]{0,2,1:T(8,128)(2,1)S(1)} %get-tuple-element.35, bf16[512,16,8]{0,2,1:T(8,128)(2,1)S(1)} %get-tuple-element.34), kind=kOutput, calls=%fused_computation.119 | convolution fusion | flops 1081081856 | bytes 36700160 | tf_op jit(solution)/shard_map/qhe,khe->hqk/dot_general | solution.py:128
  216.1 38.1 %fusion.139 = (f32[16,512]{1,0:T(8,128)S(1)}, f32[16,512,1024]{2,1,0:T(8,128)}) fusion(f32[16,512,1024]{2,1,0:T(8,128)} %fusion.104, pred[512,1024]{1,0:T(8,128)(4,1)} %compare_and_fusion), kind=kOutput, calls=%fused_computation.189 | output fusion | flops 50332672 | bytes 67665920 | tf_op jit(solution)/shard_map/sub | solution.py:135
  254.2 15.2 fusion.98
  272.6 12.1 convert_reduce_fusion.3
  291.9 14.9 fusion.75
  306.9 22.4 %multiply_reduce_fusion = (f32[16,512]{1,0:T(8,128)S(1)}, f32[16,512,1024]{2,1,0:T(8,128)}) fusion(f32[16,512,1024]{2,1,0:T(8,128)} %get-tuple-element.57, f32[16,512]{1,0:T(8,128)S(1)} %get-tuple-element.56, bf16[512,16,64]{0,2,1:T(8,128)(2,1)S(1)} %bitcast.119, bf16[1024,16,64]{0,2,1:T(8,128)(2,1)S(1)} %bitcast.115), kind=kOutput, calls=%fused_computation.3 | convolution fusion | flops 1098899456 | bytes 70320128 | tf_op jit(solution)/shard_map/qhe,khe->hqk/dot_general | solution.py:165
  329.3 8.1 fusion.141
  338.9 28.0 %multiply_convert_fusion = bf16[16,512,1024]{2,1,0:T(8,128)(2,1)} fusion(f32[16,512,1024]{2,1,0:T(8,128)} %get-tuple-element.61, f32[16,512]{1,0:T(8,128)S(1)} %get-tuple-element.60, f32[16,512,1024]{2,1,0:T(8,128)} %get-tuple-element.57, f32[16,512]{1,0:T(8,128)S(1)} %get-tuple-element.56), kind=kLoop, calls=%fused_computation.2 | loop fusion | flops 33554432 | bytes 83951616 | tf_op jit(solution)/shard_map/convert_element_type | solution.py:169
  366.9 9.1 multiply_bitcast_fusion.2
  378.4 13.2 convert_reduce_fusion
  393.6 8.6 fusion.122
  402.2 12.9 multiply_bitcast_fusion.3
  429.4 9.8 fusion.125
  439.2 33.4 %pad_maximum_fusion = f32[1024,12288]{1,0:T(8,128)} fusion(f32[1024,4096]{1,0:T(8,128)} %fusion.141, f32[1024,4096]{1,0:T(8,128)} %fusion.122, f32[1024,1024]{1,0:T(8,128)} %fusion.140, f32[1024,3072]{1,0:T(8,128)} %fusion.125), kind=kLoop, calls=%fused_computation.1 | loop fusion | flops 37748736 | bytes 100663296 | tf_op jit(solution)/shard_map/concatenate | solution.py:212
  472.7 820.8 %reduce-scatter.3.cloned.1.call-done = f32[1024,3072]{1,0:T(8,128)} async-done(((f32[1024,12288]{1,0:T(8,128)}), f32[1024,3072]{1,0:T(8,128)}) %reduce-scatter.3.cloned.1.call-update) | async-done | bytes 12582928 | tf_op jit(solution)/shard_map/reduce_scatter | solution.py:223
  1293.6 98.3 %reduce-scatter.5.cloned.1.call-done = f32[128,3072]{1,0:T(8,128)} async-done(((f32[1024,3072]{1,0:T(8,128)}), f32[128,3072]{1,0:T(8,128)}) %reduce-scatter.5.cloned.1.call-update) | async-done | bytes 1572880 | tf_op jit(solution)/shard_map/reduce_scatter | solution.py:227
  1395.1 8.6 fusion.19
  1403.7 7.9 fusion.131
  1415.1 21.5 %all-reduce.7 = f32[13312]{0:T(1024)S(1)} all-reduce(f32[13312]{0:T(1024)S(1)} %reshape.306), channel_id=4, replica_groups=mesh['dp'=4,'shard'=8] {'dp'}, use_global_device_ids=true, to_apply=%region_21.22.clone | all-reduce | flops 13312 | bytes 106496
  1436.7 25.6 %all-reduce.8 = f32[3328]{0:T(1024)S(1)} all-reduce(f32[3328]{0:T(1024)S(1)} %dynamic-slice.2), channel_id=5, replica_groups=mesh['dp'=4,'shard'=8] {'shard'}, use_global_device_ids=true, to_apply=%region_22.23.clone | all-reduce | flops 3328 | bytes 26624
  1462.4 11.3 all-reduce.6
  1474.3 37.0 %all-gather.6.cloned.1.call-done = f32[128,12288]{1,0:T(8,128)} async-done(((f32[128,3072]{1,0:T(8,128)}), f32[128,12288]{1,0:T(8,128)}) %all-gather.6.cloned.1.call-update) | async-done | bytes 6291472 | tf_op jit(solution)/shard_map/all_gather | solution.py:231
  1522.4 14.7 psum.15
  1548.2 6.6 copy.73
  1554.8 18.9 %fusion.28 = f32[1,96,128,128]{3,2,1,0:T(8,128)} fusion(f32[1,96,128,128]{3,2,1,0:T(8,128)} %param.17, f32[16,96,8,128]{3,2,1,0:T(8,128)} %get-tuple-element.27), kind=kOutput, calls=%fused_computation.48 | convolution fusion | flops 2419064832 | bytes 18874368 | tf_op jit(solution)/shard_map/iajb,icjb->ijac/dot_general | solution.py:239
  1573.7 11.6 fusion.27
  1585.3 9.7 broadcast_multiply_fusion
  1601.6 9.3 fusion.133
  (209 shorter events, 106.8 us)
Async XLA Ops:
  7.2 1578.1 %copy-start = (bf16[1,96,128,128]{3,2,1,0:T(8,128)(2,1)S(1)}, bf16[1,96,128,128]{3,2,1,0:T(8,128)(2,1)}, u32[]{:S(2)}) copy-start(bf16[1,96,128,128]{3,2,1,0:T(8,128)(2,1)} %param.20) | copy-start | bytes 9437188
  7.2 48.3 %copy-start.36 = (f32[1664]{0:T(1024)S(1)}, f32[1664]{0:T(1024)}, u32[]{:S(2)}) copy-start(f32[1664]{0:T(1024)} %param.16) | copy-start | bytes 19972
  7.2 134.2 %all-gather.4.cloned.1.call-start = ((), (), s32[]{:S(2)}) async-start(), calls=%async_computation.2 | async-start | bytes 28311552 | tf_op jit(solution)/shard_map/all_gather | solution.py:81
  12.3 1281.2 %reduce-scatter.3.cloned.1.call-start = ((), (), s32[]{:S(2)}) async-start(), calls=%async_computation.3 | async-start | bytes 62914560 | tf_op jit(solution)/shard_map/reduce_scatter | solution.py:223
  65.7 92.6 %copy-start.42 = (f32[4096]{0:T(1024)}, f32[4096]{0:T(1024)S(1)}, u32[]{:S(2)}) copy-start(f32[4096]{0:T(1024)S(1)} %slice.122) | copy-start | bytes 49156
  68.8 89.6 %copy-start.34 = (f32[512]{0:T(512)}, f32[512]{0:T(512)S(1)}, u32[]{:S(2)}) copy-start(f32[512]{0:T(512)S(1)} %broadcast_multiply_fusion.1) | copy-start | bytes 6148
  71.4 87.0 %copy-start.38 = (f32[512]{0:T(512)}, f32[512]{0:T(512)S(1)}, u32[]{:S(2)}) copy-start(f32[512]{0:T(512)S(1)} %fusion.115) | copy-start | bytes 6148
  72.6 75.0 %copy-start.32 = (f32[1024]{0:T(1024)}, f32[1024]{0:T(1024)S(1)}, u32[]{:S(2)}) copy-start(f32[1024]{0:T(1024)S(1)} %get-tuple-element.45) | copy-start | bytes 12292
  72.6 75.0 %copy-start.47 = (f32[1024]{0:T(1024)}, f32[1024]{0:T(1024)S(1)}, u32[]{:S(2)}) copy-start(f32[1024]{0:T(1024)S(1)} %get-tuple-element.44) | copy-start | bytes 12292
  72.6 85.8 %copy-start.30 = (f32[1024]{0:T(1024)}, f32[1024]{0:T(1024)S(1)}, u32[]{:S(2)}) copy-start(f32[1024]{0:T(1024)S(1)} %get-tuple-element.43) | copy-start | bytes 12292
  72.6 85.8 %copy-start.49 = (f32[1024]{0:T(1024)}, f32[1024]{0:T(1024)S(1)}, u32[]{:S(2)}) copy-start(f32[1024]{0:T(1024)S(1)} %get-tuple-element.42) | copy-start | bytes 12292
  72.7 117.6 %copy-start.26 = (f32[512,8]{0,1:T(8,128)}, f32[512,8]{0,1:T(8,128)S(1)}, u32[]{:S(2)}) copy-start(f32[512,8]{0,1:T(8,128)S(1)} %get-tuple-element.50) | copy-start | bytes 49156
  72.7 117.6 %copy-start.28 = (f32[512,8]{0,1:T(8,128)}, f32[512,8]{0,1:T(8,128)S(1)}, u32[]{:S(2)}) copy-start(f32[512,8]{0,1:T(8,128)S(1)} %get-tuple-element.51) | copy-start | bytes 49156
  151.2 40.2 %collective-permute-start = (bf16[512,1024]{1,0:T(8,128)(2,1)}, bf16[512,1024]{1,0:T(8,128)(2,1)}, u32[]{:S(2)}, u32[]{:S(2)}) collective-permute-start(bf16[512,1024]{1,0:T(8,128)(2,1)} %slice.167), channel_id=1, source_target_pairs={{0,1},{1,0},{2,3},{3,2},{4,5},{5,4},{6,7},{7,6},{8,9},{9,8},{10,11... | collective-permute-start | bytes 3145736 | tf_op jit(solution)/shard_map/ppermute | solution.py:19
  158.1 40.5 %collective-permute-start.1 = (bf16[512,1024]{0,1:T(8,128)(2,1)}, bf16[512,1024]{0,1:T(8,128)(2,1)}, u32[]{:S(2)}, u32[]{:S(2)}) collective-permute-start(bf16[512,1024]{0,1:T(8,128)(2,1)} %bitcast.4), channel_id=1, source_target_pairs={{0,1},{1,0},{2,3},{3,2},{4,5},{5,4},{6,7},{7,6},{8,9},{9,8},{10,11... | collective-permute-start | bytes 3145736 | tf_op jit(solution)/shard_map/ppermute | solution.py:19
  191.4 24.6 %copy-start.18 = (bf16[512,16,8]{0,2,1:T(8,128)(2,1)}, bf16[512,16,8]{0,2,1:T(8,128)(2,1)S(1)}, u32[]{:S(2)}) copy-start(bf16[512,16,8]{0,2,1:T(8,128)(2,1)S(1)} %get-tuple-element.34) | copy-start | bytes 393220
  191.4 24.6 %copy-start.20 = (bf16[512,16,8]{0,2,1:T(8,128)(2,1)}, bf16[512,16,8]{0,2,1:T(8,128)(2,1)S(1)}, u32[]{:S(2)}) copy-start(bf16[512,16,8]{0,2,1:T(8,128)(2,1)S(1)} %get-tuple-element.35) | copy-start | bytes 393220
  254.2 18.4 %copy-start.51 = (f32[1024]{0:T(1024)S(1)}, f32[1024]{0:T(1024)}, u32[]{:S(2)}) copy-start(f32[1024]{0:T(1024)} %get-tuple-element.40) | copy-start | bytes 12292
  254.2 18.4 %copy-start.52 = (f32[1024]{0:T(1024)S(1)}, f32[1024]{0:T(1024)}, u32[]{:S(2)}) copy-start(f32[1024]{0:T(1024)} %get-tuple-element.41) | copy-start | bytes 12292
  254.2 18.4 %copy-start.54 = (f32[512]{0:T(512)S(1)}, f32[512]{0:T(512)}, u32[]{:S(2)}) copy-start(f32[512]{0:T(512)} %convert_multiply_fusion) | copy-start | bytes 6148
  306.8 22.5 %copy-start.16 = (bf16[512,4096]{1,0:T(8,128)(2,1)S(1)}, bf16[512,4096]{1,0:T(8,128)(2,1)}, u32[]{:S(2)}) copy-start(bf16[512,4096]{1,0:T(8,128)(2,1)} %get-tuple-element.24) | copy-start | bytes 12582916
  306.9 22.5 %copy-start.24 = (bf16[512,1024]{1,0:T(8,128)(2,1)S(1)}, bf16[512,1024]{1,0:T(8,128)(2,1)}, u32[]{:S(2)}) copy-start(bf16[512,1024]{1,0:T(8,128)(2,1)} %copy-done.23) | copy-start | bytes 3145732
  338.6 86.2 %collective-permute-start.3 = (bf16[512,1024]{0,1:T(8,128)(2,1)}, bf16[512,1024]{0,1:T(8,128)(2,1)}, u32[]{:S(2)}, u32[]{:S(2)}) collective-permute-start(bf16[512,1024]{0,1:T(8,128)(2,1)} %bitcast.18), channel_id=1, source_target_pairs={{0,1},{1,0},{2,3},{3,2},{4,5},{5,4},{6,7},{7,6},{8,9},{9,8},{10,11... | collective-permute-start | bytes 3145736 | tf_op jit(solution)/shard_map/ppermute | solution.py:19
  338.9 28.0 %copy-start.19 = (bf16[512,16,8]{0,2,1:T(8,128)(2,1)S(1)}, bf16[512,16,8]{0,2,1:T(8,128)(2,1)}, u32[]{:S(2)}) copy-start(bf16[512,16,8]{0,2,1:T(8,128)(2,1)} %copy-done.18) | copy-start | bytes 393220
  338.9 28.0 %copy-start.21 = (bf16[512,16,8]{0,2,1:T(8,128)(2,1)S(1)}, bf16[512,16,8]{0,2,1:T(8,128)(2,1)}, u32[]{:S(2)}) copy-start(bf16[512,16,8]{0,2,1:T(8,128)(2,1)} %copy-done.20) | copy-start | bytes 393220
  377.3 42.8 %collective-permute-start.2 = (bf16[512,1024]{0,1:T(8,128)(2,1)}, bf16[512,1024]{0,1:T(8,128)(2,1)}, u32[]{:S(2)}, u32[]{:S(2)}) collective-permute-start(bf16[512,1024]{0,1:T(8,128)(2,1)} %bitcast.13), channel_id=1, source_target_pairs={{0,1},{1,0},{2,3},{3,2},{4,5},{5,4},{6,7},{7,6},{8,9},{9,8},{10,11... | collective-permute-start | bytes 3145736 | tf_op jit(solution)/shard_map/ppermute | solution.py:19
  378.3 15.2 copy-start.31
  472.7 919.2 %reduce-scatter.5.cloned.1.call-start = ((), (), s32[]{:S(2)}) async-start(), calls=%async_computation.4 | async-start | bytes 14155776 | tf_op jit(solution)/shard_map/reduce_scatter | solution.py:227
  1293.5 98.4 %copy-start.55 = (u32[32]{0:T(128)S(1)}, u32[32]{0:T(128)}, u32[]{:S(2)}) copy-start(u32[32]{0:T(128)} %constant.199) | copy-start | bytes 388
  1293.5 99.0 %copy-start.53 = (u32[32]{0:T(128)S(1)}, u32[32]{0:T(128)}, u32[]{:S(2)}) copy-start(u32[32]{0:T(128)} %constant.189) | copy-start | bytes 388
  1293.5 217.8 %all-gather.6.cloned.1.call-start = ((), (), s32[]{:S(2)}) async-start(), calls=%async_computation.5 | async-start | bytes 7864320 | tf_op jit(solution)/shard_map/all_gather | solution.py:231
  1554.8 18.9 %copy-start.1 = (f32[128,96,128]{0,2,1:T(8,128)S(1)}, f32[128,96,128]{0,2,1:T(8,128)}, u32[]{:S(2)}) copy-start(f32[128,96,128]{0,2,1:T(8,128)} %copy.73) | copy-start | bytes 18874372
  (36 other events, 253.3 us)
Sparse Core Ops, SparseCore 0:
  12.4 129.0 all-gather.3
  472.8 820.6 reduce-scatter.2
  1297.4 94.4 reduce-scatter.4
  1393.4 117.8 all-gather.5
where the time goes:
time: 1630 us; the launch traced here: 1620 us
  waiting for transfers between devices  1020 us (63%)
  matrix products  245 us (15%)
  other arithmetic  151 us (9%)
  blocking collectives  126 us (8%)
  local copies, waits for them, and re-layouts  52.1 us (3%)
  between operations  20.6 us (1%)
    reduce_scatter x1, waiting for transfers between devices, body(): lax.psum_scatter(weight_grad, 'dp', scatter_dimension=1, tiled=True)  821 us
    reduce_scatter x1, waiting for transfers between devices, body(): lax.psum_scatter(part_weight, 'shard', scatter_dimension=0, tiled=True)  98.3 us
    all_gather x1, waiting for transfers between devices, body(): lax.all_gather(master.astype(jnp.bfloat16), 'shard', axis=0, tiled=True)  67.4 us
    unnamed x3, blocking collectives  58.4 us
    psum x1, blocking collectives, body(): valid_total = lax.psum(jnp.sum(valid_float), ('dp', 'shard'))  42.6 us
    sub x1, other arithmetic, body(): exponent = jnp.exp(scores - row_max)  38.1 us
    all_gather x1, waiting for transfers between devices, body(): lax.all_gather(part_weight, 'dp', axis=1, tiled=True)  37 us
    concatenate x1, other arithmetic, body(): jnp.concatenate([jnp.einsum('td,tc->dc', one_low, qkv_low, preferred_elem...  33.4 us
  transfers between devices with their start and end apart: 8, of which 4 were waited for; matrix products, arithmetic and copies ran while one was open for 10% of the time, Pallas kernels for 0%

commit v1 on v0

--- a/solution.py
+++ b/solution.py
@@ -1,3 +1,4 @@
+import functools
 from functools import partial
 import math
 import jax
@@ -13,6 +14,36 @@
 LEARN = 0.5
 LEARN_VEC = 0.15
 HIGHEST = lax.Precision.HIGHEST
+
+
+def _divide_group(u, axis_no):
+    step_out = list(u.shape[1:])
+    step_out[axis_no] *= u.shape[0]
+    x_new = jnp.moveaxis(u, 0, axis_no).reshape(step_out)
+    return x_new
+
+
+def post_the_panels(my_tile, axis_key):
+    n_parts = lax.axis_size(axis_key)
+    main = my_tile[None]
+    for num in range(n_parts.bit_length() - 1):
+        vec_out = 1 << num
+        tray = []
+        for j in range(n_parts):
+            tray.append((j, j ^ vec_out))
+        value_now = lax.ppermute(main, axis_name=axis_key, perm=tray)
+        w_next = jnp.stack([main, value_now])
+        res = lax.axis_index(axis_key) >> num & 1
+        main = jnp.where(res == 0, w_next, w_next[::-1]).reshape(-1, *my_tile.shape)
+    return main
+
+
+def raise_lines_up(u_in, buf, d_out):
+    heard = _divide_group(post_the_panels(u_in, buf), d_out)
+    return heard
+
+
+register_patch = functools.partial(raise_lines_up, buf="shard", d_out=0)
 
 
 def partner(shard, axis, distance):
@@ -78,7 +109,7 @@
     is_later = shard_index % 2
     partner_index = shard_index + 1 - 2 * is_later
     weights, vector_copy = (
-        lax.all_gather(master.astype(jnp.bfloat16), "shard", axis=0, tiled=True),
+        register_patch(master.astype(jnp.bfloat16)),
         lax.all_gather(vectors.astype(jnp.bfloat16), "shard", axis=0, tiled=True),
     )
     valid_float = valid.astype(jnp.float32)

time: 1630 us -> 2020 us (1.24)
  blocking collectives: 126 us -> 387 us
  waiting for transfers between devices: 1020 us -> 1100 us
  other arithmetic: 151 us -> 210 us
    psum x1, blocking collectives: 42.6 us -> 304 us  [body(): valid_total = lax.psum(jnp.sum(valid_float), ('dp', 'shard'))]
    ppermute x0 -> x3, waiting for transfers between devices: none -> 142 us  [post_the_panels(): value_now = lax.ppermute(main, axis_name=axis_key, perm=tray)]
    all_gather x1 -> x0, waiting for transfers between devices: 67.4 us -> none  [body(): lax.all_gather(master.astype(jnp.bfloat16), 'shard', axis=0, tiled=True)]
    another operation x4 -> x9, other arithmetic: 3.13 us -> 46.1 us  [the longest x5 42.9 us: post_the_panels(): w_next = jnp.stack([main, value_now])]
    select_n x0 -> x2, other arithmetic: none -> 21.4 us  [post_the_panels(): main = jnp.where(res == 0, w_next, w_next[::-1]).reshape(-1, *my_tile.shape)]
  transfers between devices with their start and end apart: 8 -> 10, of which waited for: 4 -> 5; matrix products, arithmetic and copies ran while one was open for 10% -> 8% of each run, Pallas kernels for 0% -> 0%
where the time goes in v1:
time: 2020 us
  waiting for transfers between devices  1100 us (54%)
  blocking collectives  387 us (19%)
  matrix products  246 us (12%)
  other arithmetic  210 us (10%)
  local copies, waits for them, and re-layouts  52.1 us (3%)
  between operations  20.7 us (1%)
    reduce_scatter x1, waiting for transfers between devices, body(): lax.psum_scatter(weight_grad, 'dp', scatter_dimension=1, tiled=True)  819 us
    psum x1, blocking collectives, body(): valid_total = lax.psum(jnp.sum(valid_float), ('dp', 'shard'))  304 us
    ppermute x3, waiting for transfers between devices, post_the_panels(): value_now = lax.ppermute(main, axis_name=axis_key, perm=tray)  142 us
    reduce_scatter x1, waiting for transfers between devices, body(): lax.psum_scatter(part_weight, 'shard', scatter_dimension=0, tiled=True)  98.3 us
    unnamed x3, blocking collectives  58.3 us
    another operation x5, other arithmetic, post_the_panels(): w_next = jnp.stack([main, value_now])  42.9 us
  transfers between devices with their start and end apart: 10, of which 5 were waited for; matrix products, arithmetic and copies ran while one was open for 8% of the time, Pallas kernels for 0%

profile of v1, /device:TPU:0, one launch (start us, length us, event | category | flops | bytes accessed | tf_op | source)
XLA Modules:
  0.0 2017.5 jit_solution(4784482321051394474)
XLA Ops:
  25.9 12.3 fusion.36
  41.0 136.1 %collective-permute-done.1 = bf16[2,128,12288]{2,1,0:T(8,128)(2,1)} collective-permute-done((bf16[2,128,12288]{2,1,0:T(8,128)(2,1)}, bf16[2,128,12288]{2,1,0:T(8,128)(2,1)}, u32[]{:S(2)}, u32[]{:S(2)}) %collective-permute-start.1) | collective-permute-done | bytes 6291488 | tf_op jit(solution)/shard_map/ppermute | solution.py:34
  193.1 304.2 %psum.14 = f32[]{:T(128)} all-reduce(f32[]{:T(128)} %convert_reduce_fusion.4), channel_id=1, replica_groups=mesh['dp'=4,'shard'=8] {'dp','shard'}, use_global_device_ids=true, to_apply=%region_1.2 | all-reduce | flops 1 | bytes 8 | tf_op jit(solution)/shard_map/psum | solution.py:116
  497.3 10.1 all-gather
  515.4 11.9 pad_maximum_fusion.1
  527.4 14.0 reverse_select_fusion
  558.1 26.6 %multiply_convert_fusion.1 = (bf16[512,4096]{1,0:T(8,128)(2,1)}, f32[512,4096]{1,0:T(8,128)}, f32[512,4096]{1,0:T(8,128)}) fusion(f32[4096]{0:T(1024)S(1)} %slice.122, bf16[1024,12288]{1,0:T(8,128)(2,1)} %bitcast.115, bf16[512,1024]{1,0:T(8,128)(2,1)} %param.11, f32[1024]{0:T(1024)S(1)} %get-tuple-element.46, f32[1024]{0:T(1024)S(1)} %get-tuple-element.47, ...), kind=kOutput, calls=%fused_computation.20 | convolution fusion | flops 4436525056 | bytes 30437376 | tf_op jit(solution)/shard_map/dot_general | solution.py:177
  598.4 17.4 fusion.106
  615.8 38.2 %fusion.141 = (f32[16,512]{1,0:T(8,128)S(1)}, f32[16,512,1024]{2,1,0:T(8,128)}) fusion(f32[16,512,1024]{2,1,0:T(8,128)} %fusion.106, pred[512,1024]{1,0:T(8,128)(4,1)} %compare_and_fusion), kind=kOutput, calls=%fused_computation.199 | output fusion | flops 50332672 | bytes 67665920 | tf_op jit(solution)/shard_map/sub | solution.py:166
  654.0 15.4 fusion.100
  672.6 12.2 convert_reduce_fusion.3
  692.0 14.9 fusion.77
  706.9 22.4 %multiply_reduce_fusion = (f32[16,512]{1,0:T(8,128)S(1)}, f32[16,512,1024]{2,1,0:T(8,128)}) fusion(f32[16,512,1024]{2,1,0:T(8,128)} %get-tuple-element.61, f32[16,512]{1,0:T(8,128)S(1)} %get-tuple-element.60, bf16[512,16,64]{0,2,1:T(8,128)(2,1)S(1)} %bitcast.141, bf16[1024,16,64]{0,2,1:T(8,128)(2,1)S(1)} %bitcast.137), kind=kOutput, calls=%fused_computation.4 | convolution fusion | flops 1098899456 | bytes 70320128 | tf_op jit(solution)/shard_map/qhe,khe->hqk/dot_general | solution.py:196
  739.1 27.7 %multiply_convert_fusion = bf16[16,512,1024]{2,1,0:T(8,128)(2,1)} fusion(f32[16,512,1024]{2,1,0:T(8,128)} %get-tuple-element.65, f32[16,512]{1,0:T(8,128)S(1)} %get-tuple-element.64, f32[16,512,1024]{2,1,0:T(8,128)} %get-tuple-element.61, f32[16,512]{1,0:T(8,128)S(1)} %get-tuple-element.60), kind=kLoop, calls=%fused_computation.3 | loop fusion | flops 33554432 | bytes 83951616 | tf_op jit(solution)/shard_map/convert_element_type | solution.py:200
  766.9 9.1 multiply_bitcast_fusion.2
  778.4 13.2 convert_reduce_fusion
  793.6 8.8 fusion.124
  802.4 12.9 multiply_bitcast_fusion.3
  829.6 9.8 fusion.127
  839.3 33.2 %pad_maximum_fusion = f32[1024,12288]{1,0:T(8,128)} fusion(f32[1024,4096]{1,0:T(8,128)} %fusion.143, f32[1024,4096]{1,0:T(8,128)} %fusion.124, f32[1024,1024]{1,0:T(8,128)} %fusion.142, f32[1024,3072]{1,0:T(8,128)} %fusion.127), kind=kLoop, calls=%fused_computation.1 | loop fusion | flops 37748736 | bytes 100663296 | tf_op jit(solution)/shard_map/concatenate | solution.py:243
  872.6 819.0 %reduce-scatter.3.cloned.1.call-done = f32[1024,3072]{1,0:T(8,128)} async-done(((f32[1024,12288]{1,0:T(8,128)}), f32[1024,3072]{1,0:T(8,128)}) %reduce-scatter.3.cloned.1.call-update) | async-done | bytes 12582928 | tf_op jit(solution)/shard_map/reduce_scatter | solution.py:254
  1691.7 98.3 %reduce-scatter.5.cloned.1.call-done = f32[128,3072]{1,0:T(8,128)} async-done(((f32[1024,3072]{1,0:T(8,128)}), f32[128,3072]{1,0:T(8,128)}) %reduce-scatter.5.cloned.1.call-update) | async-done | bytes 1572880 | tf_op jit(solution)/shard_map/reduce_scatter | solution.py:258
  1793.2 8.8 fusion.19
  1813.4 21.5 %all-reduce.7 = f32[13312]{0:T(1024)S(1)} all-reduce(f32[13312]{0:T(1024)S(1)} %reshape.314), channel_id=4, replica_groups=mesh['dp'=4,'shard'=8] {'dp'}, use_global_device_ids=true, to_apply=%region_21.22.clone | all-reduce | flops 13312 | bytes 106496
  1835.0 25.0 %all-reduce.8 = f32[3328]{0:T(1024)S(1)} all-reduce(f32[3328]{0:T(1024)S(1)} %dynamic-slice.2), channel_id=5, replica_groups=mesh['dp'=4,'shard'=8] {'shard'}, use_global_device_ids=true, to_apply=%region_22.23.clone | all-reduce | flops 3328 | bytes 26624
  1860.2 11.8 all-reduce.6
  1872.6 37.0 %all-gather.3.cloned.1.call-done = f32[128,12288]{1,0:T(8,128)} async-done(((f32[128,3072]{1,0:T(8,128)}), f32[128,12288]{1,0:T(8,128)}) %all-gather.3.cloned.1.call-update) | async-done | bytes 6291472 | tf_op jit(solution)/shard_map/all_gather | solution.py:262
  1920.7 14.4 psum.15
  1952.9 18.9 fusion.28
  1971.8 11.6 fusion.27
  1983.4 9.7 broadcast_multiply_fusion
  1999.7 9.3 fusion.135
  (220 shorter events, 160.8 us)
Async XLA Ops:
  7.2 1976.2 %copy-start = (bf16[1,96,128,128]{3,2,1,0:T(8,128)(2,1)S(1)}, bf16[1,96,128,128]{3,2,1,0:T(8,128)(2,1)}, u32[]{:S(2)}) copy-start(bf16[1,96,128,128]{3,2,1,0:T(8,128)(2,1)} %param.20) | copy-start | bytes 9437188
  7.2 1684.4 %reduce-scatter.3.cloned.1.call-start = ((), (), s32[]{:S(2)}) async-start(), calls=%async_computation.2 | async-start | bytes 62914560 | tf_op jit(solution)/shard_map/reduce_scatter | solution.py:254
  13.7 6.1 collective-permute-start
  38.2 139.0 %collective-permute-start.1 = (bf16[2,128,12288]{2,1,0:T(8,128)(2,1)}, bf16[2,128,12288]{2,1,0:T(8,128)(2,1)}, u32[]{:S(2)}, u32[]{:S(2)}) collective-permute-start(bf16[2,128,12288]{2,1,0:T(8,128)(2,1)} %get-tuple-element.31), channel_id=1, source_target_pairs={{0,2},{1,3},{2,0},{3,1},{4,6},{5,7},{6,4},{7,5},{8,10},{9,11},{10,... | collective-permute-start | bytes 18874376 | tf_op jit(solution)/shard_map/ppermute | solution.py:34
  183.3 314.0 %copy-start.37 = (f32[1664]{0:T(1024)S(1)}, f32[1664]{0:T(1024)}, u32[]{:S(2)}) copy-start(f32[1664]{0:T(1024)} %param.16) | copy-start | bytes 19972
  190.7 324.7 %collective-permute-start.2 = (bf16[4,128,12288]{2,1,0:T(8,128)(2,1)}, bf16[4,128,12288]{2,1,0:T(8,128)(2,1)}, u32[]{:S(2)}, u32[]{:S(2)}) collective-permute-start(bf16[4,128,12288]{2,1,0:T(8,128)(2,1)} %bitcast.8), channel_id=1, source_target_pairs={{0,4},{1,5},{2,6},{3,7},{4,0},{5,1},{6,2},{7,3},{8,12},{9,13},{10,... | collective-permute-start | bytes 37748744 | tf_op jit(solution)/shard_map/ppermute | solution.py:34
  507.5 50.6 %copy-start.43 = (f32[4096]{0:T(1024)}, f32[4096]{0:T(1024)S(1)}, u32[]{:S(2)}) copy-start(f32[4096]{0:T(1024)S(1)} %slice.122) | copy-start | bytes 49156
  510.6 47.5 %copy-start.35 = (f32[512]{0:T(512)}, f32[512]{0:T(512)S(1)}, u32[]{:S(2)}) copy-start(f32[512]{0:T(512)S(1)} %broadcast_multiply_fusion.1) | copy-start | bytes 6148
  512.8 45.3 %copy-start.39 = (f32[512]{0:T(512)}, f32[512]{0:T(512)S(1)}, u32[]{:S(2)}) copy-start(f32[512]{0:T(512)S(1)} %fusion.117) | copy-start | bytes 6148
  514.0 27.4 %copy-start.33 = (f32[1024]{0:T(1024)}, f32[1024]{0:T(1024)S(1)}, u32[]{:S(2)}) copy-start(f32[1024]{0:T(1024)S(1)} %get-tuple-element.49) | copy-start | bytes 12292
  514.0 27.4 %copy-start.48 = (f32[1024]{0:T(1024)}, f32[1024]{0:T(1024)S(1)}, u32[]{:S(2)}) copy-start(f32[1024]{0:T(1024)S(1)} %get-tuple-element.48) | copy-start | bytes 12292
  514.0 44.1 %copy-start.31 = (f32[1024]{0:T(1024)}, f32[1024]{0:T(1024)S(1)}, u32[]{:S(2)}) copy-start(f32[1024]{0:T(1024)S(1)} %get-tuple-element.47) | copy-start | bytes 12292
  514.0 44.1 %copy-start.50 = (f32[1024]{0:T(1024)}, f32[1024]{0:T(1024)S(1)}, u32[]{:S(2)}) copy-start(f32[1024]{0:T(1024)S(1)} %get-tuple-element.46) | copy-start | bytes 12292
  514.1 75.9 %copy-start.27 = (f32[512,8]{0,1:T(8,128)}, f32[512,8]{0,1:T(8,128)S(1)}, u32[]{:S(2)}) copy-start(f32[512,8]{0,1:T(8,128)S(1)} %get-tuple-element.54) | copy-start | bytes 49156
  514.1 75.9 %copy-start.29 = (f32[512,8]{0,1:T(8,128)}, f32[512,8]{0,1:T(8,128)S(1)}, u32[]{:S(2)}) copy-start(f32[512,8]{0,1:T(8,128)S(1)} %get-tuple-element.55) | copy-start | bytes 49156
  550.9 40.2 %collective-permute-start.3 = (bf16[512,1024]{1,0:T(8,128)(2,1)}, bf16[512,1024]{1,0:T(8,128)(2,1)}, u32[]{:S(2)}, u32[]{:S(2)}) collective-permute-start(bf16[512,1024]{1,0:T(8,128)(2,1)} %slice.167), channel_id=1, source_target_pairs={{0,1},{1,0},{2,3},{3,2},{4,5},{5,4},{6,7},{7,6},{8,9},{9,8},{10,11... | collective-permute-start | bytes 3145736 | tf_op jit(solution)/shard_map/ppermute | solution.py:50
  557.9 40.5 %collective-permute-start.4 = (bf16[512,1024]{0,1:T(8,128)(2,1)}, bf16[512,1024]{0,1:T(8,128)(2,1)}, u32[]{:S(2)}, u32[]{:S(2)}) collective-permute-start(bf16[512,1024]{0,1:T(8,128)(2,1)} %bitcast.14), channel_id=1, source_target_pairs={{0,1},{1,0},{2,3},{3,2},{4,5},{5,4},{6,7},{7,6},{8,9},{9,8},{10,11... | collective-permute-start | bytes 3145736 | tf_op jit(solution)/shard_map/ppermute | solution.py:50
  591.1 24.7 %copy-start.19 = (bf16[512,16,8]{0,2,1:T(8,128)(2,1)}, bf16[512,16,8]{0,2,1:T(8,128)(2,1)S(1)}, u32[]{:S(2)}) copy-start(bf16[512,16,8]{0,2,1:T(8,128)(2,1)S(1)} %get-tuple-element.38) | copy-start | bytes 393220
  591.1 24.7 %copy-start.21 = (bf16[512,16,8]{0,2,1:T(8,128)(2,1)}, bf16[512,16,8]{0,2,1:T(8,128)(2,1)S(1)}, u32[]{:S(2)}) copy-start(bf16[512,16,8]{0,2,1:T(8,128)(2,1)S(1)} %get-tuple-element.39) | copy-start | bytes 393220
  654.0 18.6 copy-start.53
  654.0 18.6 copy-start.55
  706.9 22.5 %copy-start.17 = (bf16[512,4096]{1,0:T(8,128)(2,1)S(1)}, bf16[512,4096]{1,0:T(8,128)(2,1)}, u32[]{:S(2)}) copy-start(bf16[512,4096]{1,0:T(8,128)(2,1)} %get-tuple-element.24) | copy-start | bytes 12582916
  706.9 22.5 %copy-start.25 = (bf16[512,1024]{1,0:T(8,128)(2,1)S(1)}, bf16[512,1024]{1,0:T(8,128)(2,1)}, u32[]{:S(2)}) copy-start(bf16[512,1024]{1,0:T(8,128)(2,1)} %copy-done.24) | copy-start | bytes 3145732
  738.8 86.2 %collective-permute-start.6 = (bf16[512,1024]{0,1:T(8,128)(2,1)}, bf16[512,1024]{0,1:T(8,128)(2,1)}, u32[]{:S(2)}, u32[]{:S(2)}) collective-permute-start(bf16[512,1024]{0,1:T(8,128)(2,1)} %bitcast.28), channel_id=1, source_target_pairs={{0,1},{1,0},{2,3},{3,2},{4,5},{5,4},{6,7},{7,6},{8,9},{9,8},{10,11... | collective-permute-start | bytes 3145736 | tf_op jit(solution)/shard_map/ppermute | solution.py:50
  739.1 27.7 %copy-start.20 = (bf16[512,16,8]{0,2,1:T(8,128)(2,1)S(1)}, bf16[512,16,8]{0,2,1:T(8,128)(2,1)}, u32[]{:S(2)}) copy-start(bf16[512,16,8]{0,2,1:T(8,128)(2,1)} %copy-done.19) | copy-start | bytes 393220
  739.1 27.7 %copy-start.22 = (bf16[512,16,8]{0,2,1:T(8,128)(2,1)S(1)}, bf16[512,16,8]{0,2,1:T(8,128)(2,1)}, u32[]{:S(2)}) copy-start(bf16[512,16,8]{0,2,1:T(8,128)(2,1)} %copy-done.21) | copy-start | bytes 393220
  777.3 42.9 %collective-permute-start.5 = (bf16[512,1024]{0,1:T(8,128)(2,1)}, bf16[512,1024]{0,1:T(8,128)(2,1)}, u32[]{:S(2)}, u32[]{:S(2)}) collective-permute-start(bf16[512,1024]{0,1:T(8,128)(2,1)} %bitcast.23), channel_id=1, source_target_pairs={{0,1},{1,0},{2,3},{3,2},{4,5},{5,4},{6,7},{7,6},{8,9},{9,8},{10,11... | collective-permute-start | bytes 3145736 | tf_op jit(solution)/shard_map/ppermute | solution.py:50
  872.6 917.4 %reduce-scatter.5.cloned.1.call-start = ((), (), s32[]{:S(2)}) async-start(), calls=%async_computation.3 | async-start | bytes 14155776 | tf_op jit(solution)/shard_map/reduce_scatter | solution.py:258
  1691.6 98.5 %copy-start.56 = (u32[32]{0:T(128)S(1)}, u32[32]{0:T(128)}, u32[]{:S(2)}) copy-start(u32[32]{0:T(128)} %constant.199) | copy-start | bytes 388
  1691.6 99.0 %copy-start.54 = (u32[32]{0:T(128)S(1)}, u32[32]{0:T(128)}, u32[]{:S(2)}) copy-start(u32[32]{0:T(128)} %constant.189) | copy-start | bytes 388
  1691.6 218.0 %all-gather.3.cloned.1.call-start = ((), (), s32[]{:S(2)}) async-start(), calls=%async_computation.4 | async-start | bytes 7864320 | tf_op jit(solution)/shard_map/all_gather | solution.py:262
  1952.9 18.9 copy-start.1
  (39 other events, 306.3 us)
Sparse Core Ops, SparseCore 0:
  872.7 818.8 reduce-scatter.2
  1695.5 94.4 reduce-scatter.4
  1791.7 117.8 all-gather.2
